TPU v7x, 32 devices: a whole 2x2x4 slice. The times are simulated.
32 devices in a mesh: row: 8 (over y, x, core), col: 4 (over z).
Axes of the slice: x: 2, y: 2, z: 4, core: 2. Of those that a mesh axis runs over, the one named last changes fastest.
Arguments:
- right_sides: float32 [64, 32768], P(None, ('row', 'col'))
- diag_tiles: float32 [32, 1024, 1024], P(('row', 'col')), as said below
- low_rank: float32 [32, 4, 8, 2, 12, 1024], P('row', 'col'), as said below
- tile_ranks: int32 [32, 4, 8], P('row', 'col'), may hold values from 1 to 12, as said below
- inv_factor: float32 [256, 8, 128, 128], P(('row', 'col')), as said below
- sub_sizes: int32 [64], replicated, may hold values from 1 to 8, 256 in all
Outputs:
- solution: float32 [64, 32768], P(None, ('row', 'col'))
- residual: float32 [64, 32768], P(None, ('row', 'col'))
Inputs may be any that keep to these rules, and one draw needn't show every extreme that they name: `low_rank`: tile (j, i) holds the two factors of tile (i, j) in swapped order, and a diagonal tile's two factors are equal, so S is symmetric. `tile_ranks`: the rank of tile (i, j) equals that of tile (j, i); diagonal tiles have rank 12. `diag_tiles`: each tile is symmetric positive definite. `inv_factor`: the block at distance 0 of every span is lower triangular with a positive diagonal. `sub_sizes`: the sizes sum to 256.
All inputs are finite; a program needn't handle non-finite values.
Results may differ from a plain program's by a relative error of at most 0.0003.
Values sent between devices are 32-bit elements; how exact they have to be, the bound alone decides.
A program may use at most 128 MiB of HBM per device.

v0:
```python
import jax
import jax.numpy as jnp
from jax import lax
from jax.sharding import PartitionSpec as P

RANK = 12
finest = lax.Precision.HIGHEST


def shifted(x, axis, by):
    size = lax.axis_size(axis)
    pairs = [(i, i + by) for i in range(size) if 0 <= i + by < size]
    return lax.ppermute(x, axis, pairs)


def span_weights(sub_sizes, per_device, reach_len):
    span_ids = lax.axis_index(("row", "col")) * per_device + lax.iota(jnp.int32, per_device)
    ending = jnp.cumsum(sub_sizes)
    opening = ending - sub_sizes
    inside = (span_ids[:, None] >= opening[None, :]) & (span_ids[:, None] < ending[None, :])
    position = span_ids - jnp.sum(jnp.where(inside, opening[None, :], 0), axis=1)
    return (lax.iota(jnp.int32, reach_len)[None, :] <= position[:, None]).astype(jnp.float32)


def precondition(vector, inv_factor, weights):
    rhs_count, tile_len = vector.shape
    per_device = inv_factor.shape[0]
    reach_len = inv_factor.shape[1]
    span_len = inv_factor.shape[2]
    before = shifted(vector, ("row", "col"), 1)
    joined = jnp.concatenate([before, vector], axis=1).reshape(rhs_count, 2 * per_device, span_len)
    windows = jnp.stack(
        [joined[:, per_device - behind : 2 * per_device - behind] for behind in range(reach_len)],
        axis=2,
    )
    windows = windows * weights[None, :, :, None]
    forward = jnp.einsum("ltji,klti->klj", inv_factor, windows, precision=finest)
    spread = (
        jnp.einsum("ltji,klj->klti", inv_factor, forward, precision=finest)
        * weights[None, :, :, None]
    )
    placed = jnp.zeros_like(joined)
    for behind in range(reach_len):
        placed = placed + jnp.pad(
            spread[:, :, behind], ((0, 0), (per_device - behind, behind), (0, 0))
        )
    returned = shifted(placed[:, :per_device].reshape(rhs_count, tile_len), ("row", "col"), -1)
    return placed[:, per_device:].reshape(rhs_count, tile_len) + returned


def operate(vector, diag_tiles, low_rank, tile_ranks):
    rhs_count, tile_len = vector.shape
    tile_rows = low_rank.shape[0]
    local_part = jnp.dot(vector, diag_tiles[0], precision=finest)
    left_factor = low_rank[:, 0, :, 0]
    right_factor = low_rank[:, 0, :, 1]
    weights = (lax.iota(jnp.int32, RANK)[None, None, :] < tile_ranks[:, 0, :, None]).astype(
        jnp.float32
    )
    initial = jnp.zeros((rhs_count, tile_rows * tile_len), jnp.float32)
    piece = lax.all_gather(vector, "row", axis=1, tiled=True)
    count_tiles = piece.shape[1] // tile_len
    pieces = piece.reshape(rhs_count, count_tiles, tile_len)
    coeffs = (
        jnp.einsum("bmqt,pmt->bmqp", right_factor, pieces, precision=finest)
        * weights[:, :, :, None]
    )
    added = jnp.einsum("bmqt,bmqp->pbt", left_factor, coeffs, precision=finest)
    partial_rows = initial + added.reshape(rhs_count, tile_rows * tile_len)
    summed = lax.psum_scatter(partial_rows, "col", scatter_dimension=1, tiled=True)
    return local_part + summed


def solve_spd(matrix, target):
    factor = jnp.linalg.cholesky(matrix)
    return jax.scipy.linalg.cho_solve((factor, True), target)


def gram_of(first_block, second_block):
    return jnp.dot(first_block, second_block.T, precision=finest)


def apply_coeffs(coeffs, block_rows):
    return jnp.dot(coeffs.T, block_rows, precision=finest)


def global_sum(terms):
    return lax.psum((terms[0], terms[1]), ("row", "col"))


def body(right_sides, diag_tiles, low_rank, tile_ranks, inv_factor, sub_sizes):
    weights = span_weights(sub_sizes, inv_factor.shape[0], inv_factor.shape[1])
    residual = right_sides
    search = precondition(residual, inv_factor, weights)
    images = operate(search, diag_tiles, low_rank, tile_ranks)
    rho_now, curvature = global_sum((gram_of(search, residual), gram_of(search, images)))
    step_size = solve_spd(curvature, rho_now)
    solution = apply_coeffs(step_size, search)
    residual = residual - apply_coeffs(step_size, images)
    precond = precondition(residual, inv_factor, weights)
    product = operate(precond, diag_tiles, low_rank, tile_ranks)
    rho_next, self_term, cross_term = lax.psum(
        (gram_of(precond, residual), gram_of(precond, product), gram_of(search, product)),
        ("row", "col"),
    )
    beta_mix = solve_spd(rho_now, rho_next)
    curvature = (
        self_term
        + jnp.dot(cross_term.T, beta_mix, precision=finest)
        + jnp.dot(beta_mix.T, cross_term, precision=finest)
        + jnp.dot(beta_mix.T, jnp.dot(curvature, beta_mix, precision=finest), precision=finest)
    )
    search = precond + apply_coeffs(beta_mix, search)
    images = product + apply_coeffs(beta_mix, images)
    step_size = solve_spd(curvature, rho_next)
    solution = solution + apply_coeffs(step_size, search)
    residual = residual - apply_coeffs(step_size, images)
    return (solution, residual)


def solution(mesh):
    placed = (
        P(None, ("row", "col")),
        P(("row", "col"), None, None),
        P("row", "col", None, None, None, None),
        P("row", "col", None),
        P(("row", "col"), None, None, None),
        P(),
    )
    return jax.shard_map(
        body,
        mesh=mesh,
        in_specs=placed,
        out_specs=(P(None, ("row", "col")), P(None, ("row", "col"))),
        check_vma=False,
    )
```

profile of v0, /device:TPU:0, one launch (start us, length us, event | category | flops | bytes accessed | tf_op | source)
XLA Modules:
  0.0 335.0 jit_solution(9789738542311892284)
XLA Ops:
  7.2 5.0 %collective-permute-start = (f32[64,1024]{1,0:T(8,128)}, f32[64,1024]{1,0:T(8,128)S(1)}, u32[]{:S(2)}, u32[]{:S(2)}) collective-permute-start(f32[64,1024]{1,0:T(8,128)} %param.9), channel_id=1, source_target_pairs={{0,1},{1,2},{2,3},{3,4},{4,5},{5,6},{6,7},{7,8},{8,9},{9,10},{10,1... | collective-permute-start | bytes 786440 | tf_op jit(solution)/shard_map/ppermute | solution.py:13
  14.1 3.9 %collective-permute-done = f32[64,1024]{1,0:T(8,128)S(1)} collective-permute-done((f32[64,1024]{1,0:T(8,128)}, f32[64,1024]{1,0:T(8,128)S(1)}, u32[]{:S(2)}, u32[]{:S(2)}) %collective-permute-start) | collective-permute-done | bytes 262176 | tf_op jit(solution)/shard_map/ppermute | solution.py:13
  21.5 4.6 %fusion.20 = f32[64,8,128,1]{2,0,3,1:T(8,128)S(1)} fusion(f32[8,8,128,128]{3,2,1,0:T(8,128)S(1)} %copy-done, f32[64,8,8,128]{3,0,2,1:T(8,128)S(1)} %fusion.62, f32[8,8]{1,0:T(8,128)S(1)} %fusion.89), kind=kOutput, calls=%fused_computation.23 | convolution fusion | flops 805830656 | bytes 6553856 | tf_op jit(solution)/shard_map/ltji,klti->klj/dot_general | solution.py:37
  30.3 8.7 %collective-permute-done.1 = f32[64,1024]{1,0:T(8,128)S(1)} collective-permute-done((f32[64,1024]{1,0:T(8,128)S(1)}, f32[64,1024]{1,0:T(8,128)S(1)}, u32[]{:S(2)}, u32[]{:S(2)}) %collective-permute-start.1) | collective-permute-done | bytes 262176 | tf_op jit(solution)/shard_map/ppermute | solution.py:13
  40.5 6.1 %fusion.91 = (f32[4,1,8,1,12,1024]{5,3,4,2,1,0:T(1,128)S(1)}, f32[4,1,8,1,12,1024]{5,3,4,2,1,0:T(1,128)S(1)}) fusion(f32[4,1,8,2,12,1024]{5,3,4,2,1,0:T(2,128)} %param.11), kind=kLoop, calls=%fused_computation.139 | loop fusion | bytes 6291456 | tf_op jit(solution)/shard_map/slice | solution.py:55
  46.6 25.1 %all-gather.3.cloned.1.call-done = f32[64,8192]{1,0:T(8,128)} async-done(((f32[64,1024]{1,0:T(8,128)}), f32[64,8192]{1,0:T(8,128)}) %all-gather.3.cloned.1.call-update) | async-done | bytes 2097168 | tf_op jit(solution)/shard_map/all_gather | solution.py:61
  82.3 25.9 %reduce-scatter.3.cloned.1.call-done = f32[64,1024]{1,0:T(8,128)} async-done(((f32[64,4096]{1,0:T(8,128)}), f32[64,1024]{1,0:T(8,128)}) %reduce-scatter.3.cloned.1.call-update) | async-done | bytes 262160 | tf_op jit(solution)/shard_map/reduce_scatter | solution.py:70
  108.2 4.9 %fusion.26 = f32[64,1024]{1,0:T(8,128)S(1)} fusion(f32[64,1024]{1,0:T(8,128)} %reduce-scatter.3.cloned.1.call-done, f32[64,1024]{1,0:T(8,128)S(1)} %copy-done.2, f32[1,1024,1024]{2,1,0:T(8,128)} %param.10), kind=kOutput, calls=%fused_computation.25 | convolution fusion | flops 805371904 | bytes 4980736 | tf_op jit(solution)/shard_map/dot_general | solution.py:54
  114.1 39.2 %all-reduce.17 = (f32[64,64]{0,1:T(8,128)S(1)}, f32[64,64]{0,1:T(8,128)S(1)}) all-reduce(f32[64,64]{0,1:T(8,128)S(1)} %fusion.95, f32[64,64]{0,1:T(8,128)S(1)} %fusion.94), channel_id=1, replica_groups=mesh['row'=8,'col'=4] {'row','col'}, use_global_device_ids=true, to_apply=%region_6.8 | all-reduce | flops 8192 | bytes 65536 | tf_op jit(solution)/shard_map/psum | solution.py:88
  153.4 5.8 %cholesky.59 = f32[64,64]{1,0:T(8,128)S(1)} custom-call(f32[64,64]{1,0:T(8,128)S(1)} %fusion.87), custom_call_target="Cholesky" | custom-call | tf_op jit(solution)/shard_map/jit(cholesky)/cholesky | solution.py:75
  161.4 5.7 %custom-call.9 = f32[1,64,64]{1,2,0:T(8,128)S(1)} custom-call(f32[1,64,64]{2,1,0:T(8,128)} %fusion.70), custom_call_target="InvertDiagBlocksLowerTriangular" | custom-call | tf_op jit(solution)/shard_map/jit(_cho_solve)/triangular_solve | solution.py:76
  168.9 3.8 %collective-permute-start.2 = (f32[64,1024]{1,0:T(8,128)S(1)}, f32[64,1024]{1,0:T(8,128)S(1)}, u32[]{:S(2)}, u32[]{:S(2)}) collective-permute-start(f32[64,1024]{1,0:T(8,128)S(1)} %convolution_subtract_fusion.1), channel_id=1, source_target_pairs={{0,1},{1,2},{2,3},{3,4},{4,5},{5,6},{6,7},{7,8},{8,9},{9,10},{10,1... | collective-permute-start | bytes 786440 | tf_op jit(solution)/shard_map/ppermute | solution.py:13
  172.7 4.7 %collective-permute-done.2 = f32[64,1024]{1,0:T(8,128)S(1)} collective-permute-done((f32[64,1024]{1,0:T(8,128)S(1)}, f32[64,1024]{1,0:T(8,128)S(1)}, u32[]{:S(2)}, u32[]{:S(2)}) %collective-permute-start.2) | collective-permute-done | bytes 262176 | tf_op jit(solution)/shard_map/ppermute | solution.py:13
  179.9 4.6 %fusion.23 = f32[64,8,128,1]{2,0,3,1:T(8,128)S(1)} fusion(f32[8,8,128,128]{3,2,1,0:T(8,128)S(1)} %copy-done.1, f32[64,8,8,128]{3,0,2,1:T(8,128)S(1)} %fusion.54, f32[8,8]{1,0:T(8,128)S(1)} %copy-done.9), kind=kOutput, calls=%fused_computation.24 | convolution fusion | flops 805830656 | bytes 6553856 | tf_op jit(solution)/shard_map/ltji,klti->klj/dot_general | solution.py:37
  188.7 9.1 %collective-permute-done.3 = f32[64,1024]{1,0:T(8,128)S(1)} collective-permute-done((f32[64,1024]{1,0:T(8,128)S(1)}, f32[64,1024]{1,0:T(8,128)S(1)}, u32[]{:S(2)}, u32[]{:S(2)}) %collective-permute-start.3) | collective-permute-done | bytes 262176 | tf_op jit(solution)/shard_map/ppermute | solution.py:13
  198.8 29.4 %all-gather.5.cloned.1.call-done = f32[64,8192]{1,0:T(8,128)} async-done(((f32[64,1024]{1,0:T(8,128)}), f32[64,8192]{1,0:T(8,128)}) %all-gather.5.cloned.1.call-update) | async-done | bytes 2097168 | tf_op jit(solution)/shard_map/all_gather | solution.py:61
  231.0 3.6 %fusion.47 = f32[4,8,12,64]{3,2,0,1:T(8,128)S(1)} fusion(f32[4,1,8,1,12,1024]{5,3,4,2,1,0:T(1,128)S(1)} %get-tuple-element.10, f32[64,8,1024,1]{2,1,0,3:T(8,128)S(1)} %bitcast.312, f32[4,8,12]{2,0,1:T(4,128)S(1)} %fusion.88), kind=kOutput, calls=%fused_computation.35 | convolution fusion | flops 302014464 | bytes 3769856 | tf_op jit(solution)/shard_map/bmqt,pmt->bmqp/dot_general | solution.py:65
  237.4 5.8 %cholesky.70 = f32[64,64]{1,0:T(8,128)S(1)} custom-call(f32[64,64]{1,0:T(8,128)S(1)} %fusion.82), custom_call_target="Cholesky" | custom-call | tf_op jit(solution)/shard_map/jit(cholesky)/cholesky | solution.py:75
  244.6 4.9 %custom-call.10 = f32[1,64,64]{1,2,0:T(8,128)S(1)} custom-call(f32[1,64,64]{2,1,0:T(8,128)S(1)} %fusion.71), custom_call_target="InvertDiagBlocksLowerTriangular" | custom-call | tf_op jit(solution)/shard_map/jit(_cho_solve)/triangular_solve | solution.py:76
  249.9 15.0 %reduce-scatter.5.cloned.1.call-done = f32[64,1024]{1,0:T(8,128)} async-done(((f32[64,4096]{1,0:T(8,128)}), f32[64,1024]{1,0:T(8,128)}) %reduce-scatter.5.cloned.1.call-update) | async-done | bytes 262160 | tf_op jit(solution)/shard_map/reduce_scatter | solution.py:70
  264.8 4.8 %fusion.29 = f32[64,1024]{1,0:T(8,128)S(1)} fusion(f32[64,1024]{1,0:T(8,128)} %reduce-scatter.5.cloned.1.call-done, f32[64,1024]{1,0:T(8,128)S(1)} %copy-done.3, f32[1,1024,1024]{2,1,0:T(8,128)} %param.10), kind=kOutput, calls=%fused_computation.26 | convolution fusion | flops 805371904 | bytes 4980736 | tf_op jit(solution)/shard_map/dot_general | solution.py:54
  270.4 40.1 %all-reduce.16 = (f32[64,64]{1,0:T(8,128)S(1)}, f32[64,64]{1,0:T(8,128)S(1)}, f32[64,64]{0,1:T(8,128)S(1)}) all-reduce(f32[64,64]{1,0:T(8,128)S(1)} %fusion.98, f32[64,64]{1,0:T(8,128)S(1)} %fusion.97, f32[64,64]{0,1:T(8,128)S(1)} %fusion.96), channel_id=1, replica_groups=mesh['row'=8,'col'=4] {'row','col'}, use_global_device_ids=true, to_apply=%region_10.13 | all-reduce | flops 12288 | bytes 98304 | tf_op jit(solution)/shard_map/psum | solution.py:102
  312.8 5.8 %cholesky.81 = f32[64,64]{1,0:T(8,128)S(1)} custom-call(f32[64,64]{1,0:T(8,128)S(1)} %fusion.77), custom_call_target="Cholesky" | custom-call | tf_op jit(solution)/shard_map/jit(cholesky)/cholesky | solution.py:75
  320.0 4.9 %custom-call.11 = f32[1,64,64]{1,2,0:T(8,128)S(1)} custom-call(f32[1,64,64]{2,1,0:T(8,128)S(1)} %fusion.72), custom_call_target="InvertDiagBlocksLowerTriangular" | custom-call | tf_op jit(solution)/shard_map/jit(_cho_solve)/triangular_solve | solution.py:76
  (119 shorter events, 48.6 us)
Async XLA Ops:
  7.2 64.6 %all-gather.3.cloned.1.call-start = ((), (), s32[]{:S(2)}) async-start(), calls=%async_computation.2 | async-start | bytes 2359296 | tf_op jit(solution)/shard_map/all_gather | solution.py:61
  7.2 10.8 %collective-permute-start = (f32[64,1024]{1,0:T(8,128)}, f32[64,1024]{1,0:T(8,128)S(1)}, u32[]{:S(2)}, u32[]{:S(2)}) collective-permute-start(f32[64,1024]{1,0:T(8,128)} %param.9), channel_id=1, source_target_pairs={{0,1},{1,2},{2,3},{3,4},{4,5},{5,6},{6,7},{7,8},{8,9},{9,10},{10,1... | collective-permute-start | bytes 786440 | tf_op jit(solution)/shard_map/ppermute | solution.py:13
  14.1 12.0 %copy-start.8 = (f32[8,8]{1,0:T(8,128)}, f32[8,8]{1,0:T(8,128)S(1)}, u32[]{:S(2)}) copy-start(f32[8,8]{1,0:T(8,128)S(1)} %fusion.89) | copy-start | bytes 772
  19.3 2.2 copy-start
  28.7 11.6 %copy-start.10 = (s32[4,1,8]{2,1,0:T(1,128)S(1)}, s32[4,1,8]{2,1,0:T(1,128)}, u32[]{:S(2)}) copy-start(s32[4,1,8]{2,1,0:T(1,128)} %param.12) | copy-start | bytes 388
  29.0 10.0 %collective-permute-start.1 = (f32[64,1024]{1,0:T(8,128)S(1)}, f32[64,1024]{1,0:T(8,128)S(1)}, u32[]{:S(2)}, u32[]{:S(2)}) collective-permute-start(f32[64,1024]{1,0:T(8,128)S(1)} %bitcast.318), channel_id=1, source_target_pairs={{1,0},{2,1},{3,2},{4,3},{5,4},{6,5},{7,6},{8,7},{9,8},{10,9},{11,1... | collective-permute-start | bytes 786440 | tf_op jit(solution)/shard_map/ppermute | solution.py:13
  39.8 68.4 %reduce-scatter.3.cloned.1.call-start = ((), (), s32[]{:S(2)}) async-start(), calls=%async_computation.3 | async-start | bytes 1310720 | tf_op jit(solution)/shard_map/reduce_scatter | solution.py:70
  79.7 1.3 copy-start.2
  80.8 147.5 %all-gather.5.cloned.1.call-start = ((), (), s32[]{:S(2)}) async-start(), calls=%async_computation.4 | async-start | bytes 2359296 | tf_op jit(solution)/shard_map/all_gather | solution.py:61
  113.1 0.7 copy-start.4
  168.9 8.6 %copy-start.6 = (f32[64,1024]{1,0:T(8,128)}, f32[64,1024]{1,0:T(8,128)S(1)}, u32[]{:S(2)}) copy-start(f32[64,1024]{1,0:T(8,128)S(1)} %convolution_subtract_fusion.1) | copy-start | bytes 786436
  168.9 8.6 %collective-permute-start.2 = (f32[64,1024]{1,0:T(8,128)S(1)}, f32[64,1024]{1,0:T(8,128)S(1)}, u32[]{:S(2)}, u32[]{:S(2)}) collective-permute-start(f32[64,1024]{1,0:T(8,128)S(1)} %convolution_subtract_fusion.1), channel_id=1, source_target_pairs={{0,1},{1,2},{2,3},{3,4},{4,5},{5,6},{6,7},{7,8},{8,9},{9,10},{10,1... | collective-permute-start | bytes 786440 | tf_op jit(solution)/shard_map/ppermute | solution.py:13
  177.7 2.2 copy-start.1
  177.8 2.2 copy-start.9
  187.4 10.4 %collective-permute-start.3 = (f32[64,1024]{1,0:T(8,128)S(1)}, f32[64,1024]{1,0:T(8,128)S(1)}, u32[]{:S(2)}, u32[]{:S(2)}) collective-permute-start(f32[64,1024]{1,0:T(8,128)S(1)} %bitcast.319), channel_id=1, source_target_pairs={{1,0},{2,1},{3,2},{4,3},{5,4},{6,5},{7,6},{8,7},{9,8},{10,9},{11,1... | collective-permute-start | bytes 786440 | tf_op jit(solution)/shard_map/ppermute | solution.py:13
  198.6 66.3 %reduce-scatter.5.cloned.1.call-start = ((), (), s32[]{:S(2)}) async-start(), calls=%async_computation.5 | async-start | bytes 1310720 | tf_op jit(solution)/shard_map/reduce_scatter | solution.py:70
  236.2 13.3 %copy-start.3 = (f32[64,1024]{1,0:T(8,128)S(1)}, f32[64,1024]{1,0:T(8,128)}, u32[]{:S(2)}) copy-start(f32[64,1024]{1,0:T(8,128)} %bitcast_add_fusion) | copy-start | bytes 786436
  236.2 13.3 %copy-start.7 = (f32[64,1024]{1,0:T(8,128)S(1)}, f32[64,1024]{1,0:T(8,128)}, u32[]{:S(2)}) copy-start(f32[64,1024]{1,0:T(8,128)} %copy-done.6) | copy-start | bytes 786436
  249.9 61.0 %copy-start.5 = (f32[64,1024]{1,0:T(8,128)S(1)}, f32[64,1024]{1,0:T(8,128)}, u32[]{:S(2)}) copy-start(f32[64,1024]{1,0:T(8,128)} %copy-done.4) | copy-start | bytes 786436
Sparse Core Ops, SparseCore 0:
  39.9 31.7 all-gather.2
  80.9 27.2 reduce-scatter.2
  198.7 29.5 all-gather.4
  237.4 27.3 reduce-scatter.4
where the time goes:
time: 341 us; the launch traced here: 335 us
  waiting for transfers between devices  122 us (36%)
  blocking collectives  79.3 us (23%)
  matrix products  43.8 us (13%)
  other arithmetic  41.8 us (12%)
  local copies, waits for them, and re-layouts  20.9 us (6%)
  between operations  14.9 us (4%)
  starting transfers between devices  12.5 us (4%)
    all_gather x2, waiting for transfers between devices, operate(): piece = lax.all_gather(vector, 'row', axis=1, tiled=True)  54.5 us
    reduce_scatter x2, waiting for transfers between devices, operate(): lax.psum_scatter(partial_rows, 'col', scatter_dimension=1, tiled=True)  40.8 us
    psum x1, blocking collectives, body(): lax.psum((gram_of(precond, residual), gram_of(precond, product), gram_of(...  40.1 us
    psum x1, blocking collectives, global_sum(): return lax.psum((terms[0], terms[1]), ('row', 'col'))  39.2 us
    ppermute x4, waiting for transfers between devices, shifted(): return lax.ppermute(x, axis, pairs)  26.4 us
    another operation x9, other arithmetic, solve_spd(): factor = jnp.linalg.cholesky(matrix)  19.7 us
    another operation x6, other arithmetic, solve_spd(): return jax.scipy.linalg.cho_solve((factor, True), target)  18 us
    ppermute x4, starting transfers between devices, shifted(): return lax.ppermute(x, axis, pairs)  11.4 us
  transfers between devices with their start and end apart: 8, of which 8 were waited for; matrix products, arithmetic and copies ran while one was open for 7% of the time, Pallas kernels for 0%

commit v1 on v0

--- a/solution.py
+++ b/solution.py
@@ -58,7 +58,7 @@
         jnp.float32
     )
     initial = jnp.zeros((rhs_count, tile_rows * tile_len), jnp.float32)
-    piece = lax.all_gather(vector, "row", axis=1, tiled=True)
+    piece = jnp.concatenate(lax.all_gather(vector, "row"), axis=1)
     count_tiles = piece.shape[1] // tile_len
     pieces = piece.reshape(rhs_count, count_tiles, tile_len)
     coeffs = (

time: 341 us -> 336 us (0.985)
  local copies, waits for them, and re-layouts: 20.9 us -> 15.2 us
    unnamed x42 -> x40, local copies, waits for them, and re-layouts: 10.7 us -> 5.16 us
where the time goes in v1:
time: 336 us; the launch traced here: 330 us
  waiting for transfers between devices  122 us (36%)
  blocking collectives  79.4 us (24%)
  matrix products  44.5 us (13%)
  other arithmetic  41.8 us (12%)
  local copies, waits for them, and re-layouts  15.2 us (5%)
  between operations  14.7 us (4%)
  starting transfers between devices  12.3 us (4%)
    all_gather x2, waiting for transfers between devices, operate(): piece = jnp.concatenate(lax.all_gather(vector, 'row'), axis=1)  54.6 us
    reduce_scatter x2, waiting for transfers between devices, operate(): lax.psum_scatter(partial_rows, 'col', scatter_dimension=1, tiled=True)  41 us
    psum x1, blocking collectives, body(): lax.psum((gram_of(precond, residual), gram_of(precond, product), gram_of(...  40 us
    psum x1, blocking collectives, global_sum(): return lax.psum((terms[0], terms[1]), ('row', 'col'))  39.4 us
    ppermute x4, waiting for transfers between devices, shifted(): return lax.ppermute(x, axis, pairs)  26.4 us
    another operation x9, other arithmetic, solve_spd(): factor = jnp.linalg.cholesky(matrix)  19.7 us
    another operation x6, other arithmetic, solve_spd(): return jax.scipy.linalg.cho_solve((factor, True), target)  18 us
    ppermute x4, starting transfers between devices, shifted(): return lax.ppermute(x, axis, pairs)  11.4 us
  transfers between devices with their start and end apart: 8, of which 8 were waited for; matrix products, arithmetic and copies ran while one was open for 7% of the time, Pallas kernels for 0%

profile of v1, /device:TPU:0, one launch (start us, length us, event | category | flops | bytes accessed | tf_op | source)
XLA Modules:
  0.0 330.1 jit_solution(17575768923699603502)
XLA Ops:
  7.2 5.0 %collective-permute-start = (f32[64,1024]{1,0:T(8,128)}, f32[64,1024]{1,0:T(8,128)S(1)}, u32[]{:S(2)}, u32[]{:S(2)}) collective-permute-start(f32[64,1024]{1,0:T(8,128)} %param.9), channel_id=1, source_target_pairs={{0,1},{1,2},{2,3},{3,4},{4,5},{5,6},{6,7},{7,8},{8,9},{9,10},{10,1... | collective-permute-start | bytes 786440 | tf_op jit(solution)/shard_map/ppermute | solution.py:13
  14.1 3.9 %collective-permute-done = f32[64,1024]{1,0:T(8,128)S(1)} collective-permute-done((f32[64,1024]{1,0:T(8,128)}, f32[64,1024]{1,0:T(8,128)S(1)}, u32[]{:S(2)}, u32[]{:S(2)}) %collective-permute-start) | collective-permute-done | bytes 262176 | tf_op jit(solution)/shard_map/ppermute | solution.py:13
  21.5 4.6 %fusion.18 = f32[64,8,128,1]{2,0,3,1:T(8,128)S(1)} fusion(f32[8,8,128,128]{3,2,1,0:T(8,128)S(1)} %copy-done, f32[64,8,8,128]{3,0,2,1:T(8,128)S(1)} %fusion.52, f32[8,8]{1,0:T(8,128)S(1)} %fusion.79), kind=kOutput, calls=%fused_computation.21 | convolution fusion | flops 805830656 | bytes 6553856 | tf_op jit(solution)/shard_map/ltji,klti->klj/dot_general | solution.py:37
  30.3 8.7 %collective-permute-done.1 = f32[64,1024]{1,0:T(8,128)S(1)} collective-permute-done((f32[64,1024]{1,0:T(8,128)S(1)}, f32[64,1024]{1,0:T(8,128)S(1)}, u32[]{:S(2)}, u32[]{:S(2)}) %collective-permute-start.1) | collective-permute-done | bytes 262176 | tf_op jit(solution)/shard_map/ppermute | solution.py:13
  40.4 6.1 %fusion.81 = (f32[4,1,8,1,12,1024]{5,3,4,2,1,0:T(1,128)S(1)}, f32[4,1,8,1,12,1024]{5,3,4,2,1,0:T(1,128)S(1)}) fusion(f32[4,1,8,2,12,1024]{5,3,4,2,1,0:T(2,128)} %param.11), kind=kLoop, calls=%fused_computation.137 | loop fusion | bytes 6291456 | tf_op jit(solution)/shard_map/slice | solution.py:55
  46.6 25.2 %all-gather.5.cloned.1.call-done = f32[512,1024]{1,0:T(8,128)} async-done(((f32[64,1024]{1,0:T(8,128)}), f32[512,1024]{1,0:T(8,128)}) %all-gather.5.cloned.1.call-update) | async-done | bytes 2097168 | tf_op jit(solution)/shard_map/all_gather | solution.py:61
  71.7 3.9 %fusion.33 = f32[4,8,12,64]{3,2,1,0:T(8,128)S(1)} fusion(f32[64,8,1024,1]{2,0,1,3:T(8,128)} %bitcast.320, f32[4,1,8,1,12,1024]{5,3,4,2,1,0:T(1,128)S(1)} %get-tuple-element.10, f32[4,8,12]{2,1,0:T(8,128)S(1)} %fusion.78), kind=kOutput, calls=%fused_computation.31 | convolution fusion | flops 302014464 | bytes 3769856 | tf_op jit(solution)/shard_map/bmqt,pmt->bmqp/dot_general | solution.py:65
  79.7 26.1 %reduce-scatter.3.cloned.1.call-done = f32[64,1024]{1,0:T(8,128)} async-done(((f32[64,4096]{1,0:T(8,128)}), f32[64,1024]{1,0:T(8,128)}) %reduce-scatter.3.cloned.1.call-update) | async-done | bytes 262160 | tf_op jit(solution)/shard_map/reduce_scatter | solution.py:70
  105.7 4.9 %fusion.24 = f32[64,1024]{1,0:T(8,128)S(1)} fusion(f32[64,1024]{1,0:T(8,128)} %reduce-scatter.3.cloned.1.call-done, f32[64,1024]{1,0:T(8,128)S(1)} %copy-done.2, f32[1,1024,1024]{2,1,0:T(8,128)} %param.10), kind=kOutput, calls=%fused_computation.23 | convolution fusion | flops 805371904 | bytes 4980736 | tf_op jit(solution)/shard_map/dot_general | solution.py:54
  111.7 39.4 %all-reduce.17 = (f32[64,64]{0,1:T(8,128)S(1)}, f32[64,64]{0,1:T(8,128)S(1)}) all-reduce(f32[64,64]{0,1:T(8,128)S(1)} %fusion.85, f32[64,64]{0,1:T(8,128)S(1)} %fusion.84), channel_id=1, replica_groups=mesh['row'=8,'col'=4] {'row','col'}, use_global_device_ids=true, to_apply=%region_6.8 | all-reduce | flops 8192 | bytes 65536 | tf_op jit(solution)/shard_map/psum | solution.py:88
  151.2 5.8 %cholesky.59 = f32[64,64]{1,0:T(8,128)S(1)} custom-call(f32[64,64]{1,0:T(8,128)S(1)} %fusion.77), custom_call_target="Cholesky" | custom-call | tf_op jit(solution)/shard_map/jit(cholesky)/cholesky | solution.py:75
  159.1 5.7 %custom-call.9 = f32[1,64,64]{1,2,0:T(8,128)S(1)} custom-call(f32[1,64,64]{2,1,0:T(8,128)} %fusion.60), custom_call_target="InvertDiagBlocksLowerTriangular" | custom-call | tf_op jit(solution)/shard_map/jit(_cho_solve)/triangular_solve | solution.py:76
  170.4 4.7 %collective-permute-done.2 = f32[64,1024]{1,0:T(8,128)S(1)} collective-permute-done((f32[64,1024]{1,0:T(8,128)S(1)}, f32[64,1024]{1,0:T(8,128)S(1)}, u32[]{:S(2)}, u32[]{:S(2)}) %collective-permute-start.2) | collective-permute-done | bytes 262176 | tf_op jit(solution)/shard_map/ppermute | solution.py:13
  177.6 4.6 %fusion.21 = f32[64,8,128,1]{2,0,3,1:T(8,128)S(1)} fusion(f32[8,8,128,128]{3,2,1,0:T(8,128)S(1)} %copy-done.1, f32[64,8,8,128]{3,0,2,1:T(8,128)S(1)} %fusion.44, f32[8,8]{1,0:T(8,128)S(1)} %copy-done.9), kind=kOutput, calls=%fused_computation.22 | convolution fusion | flops 805830656 | bytes 6553856 | tf_op jit(solution)/shard_map/ltji,klti->klj/dot_general | solution.py:37
  186.5 9.1 %collective-permute-done.3 = f32[64,1024]{1,0:T(8,128)S(1)} collective-permute-done((f32[64,1024]{1,0:T(8,128)S(1)}, f32[64,1024]{1,0:T(8,128)S(1)}, u32[]{:S(2)}, u32[]{:S(2)}) %collective-permute-start.3) | collective-permute-done | bytes 262176 | tf_op jit(solution)/shard_map/ppermute | solution.py:13
  196.6 29.4 %all-gather.7.cloned.1.call-done = f32[512,1024]{1,0:T(8,128)} async-done(((f32[64,1024]{1,0:T(8,128)}), f32[512,1024]{1,0:T(8,128)}) %all-gather.7.cloned.1.call-update) | async-done | bytes 2097168 | tf_op jit(solution)/shard_map/all_gather | solution.py:61
  226.0 3.9 %fusion.39 = f32[4,8,12,64]{3,2,1,0:T(8,128)S(1)} fusion(f32[64,8,1024,1]{2,0,1,3:T(8,128)} %bitcast.321, f32[4,1,8,1,12,1024]{5,3,4,2,1,0:T(1,128)S(1)} %get-tuple-element.10, f32[4,8,12]{2,1,0:T(8,128)S(1)} %fusion.78), kind=kOutput, calls=%fused_computation.33 | convolution fusion | flops 302014464 | bytes 3769856 | tf_op jit(solution)/shard_map/bmqt,pmt->bmqp/dot_general | solution.py:65
  232.7 5.8 %cholesky.70 = f32[64,64]{1,0:T(8,128)S(1)} custom-call(f32[64,64]{1,0:T(8,128)S(1)} %fusion.72), custom_call_target="Cholesky" | custom-call | tf_op jit(solution)/shard_map/jit(cholesky)/cholesky | solution.py:75
  239.9 4.9 %custom-call.10 = f32[1,64,64]{1,2,0:T(8,128)S(1)} custom-call(f32[1,64,64]{2,1,0:T(8,128)S(1)} %fusion.61), custom_call_target="InvertDiagBlocksLowerTriangular" | custom-call | tf_op jit(solution)/shard_map/jit(_cho_solve)/triangular_solve | solution.py:76
  245.2 15.0 %reduce-scatter.5.cloned.1.call-done = f32[64,1024]{1,0:T(8,128)} async-done(((f32[64,4096]{1,0:T(8,128)}), f32[64,1024]{1,0:T(8,128)}) %reduce-scatter.5.cloned.1.call-update) | async-done | bytes 262160 | tf_op jit(solution)/shard_map/reduce_scatter | solution.py:70
  260.1 4.8 %fusion.27 = f32[64,1024]{1,0:T(8,128)S(1)} fusion(f32[64,1024]{1,0:T(8,128)} %reduce-scatter.5.cloned.1.call-done, f32[64,1024]{1,0:T(8,128)S(1)} %copy-done.3, f32[1,1024,1024]{2,1,0:T(8,128)} %param.10), kind=kOutput, calls=%fused_computation.24 | convolution fusion | flops 805371904 | bytes 4980736 | tf_op jit(solution)/shard_map/dot_general | solution.py:54
  265.7 40.0 %all-reduce.16 = (f32[64,64]{1,0:T(8,128)S(1)}, f32[64,64]{1,0:T(8,128)S(1)}, f32[64,64]{0,1:T(8,128)S(1)}) all-reduce(f32[64,64]{1,0:T(8,128)S(1)} %fusion.88, f32[64,64]{1,0:T(8,128)S(1)} %fusion.87, f32[64,64]{0,1:T(8,128)S(1)} %fusion.86), channel_id=1, replica_groups=mesh['row'=8,'col'=4] {'row','col'}, use_global_device_ids=true, to_apply=%region_10.13 | all-reduce | flops 12288 | bytes 98304 | tf_op jit(solution)/shard_map/psum | solution.py:102
  308.1 5.8 %cholesky.81 = f32[64,64]{1,0:T(8,128)S(1)} custom-call(f32[64,64]{1,0:T(8,128)S(1)} %fusion.67), custom_call_target="Cholesky" | custom-call | tf_op jit(solution)/shard_map/jit(cholesky)/cholesky | solution.py:75
  315.3 4.9 %custom-call.11 = f32[1,64,64]{1,2,0:T(8,128)S(1)} custom-call(f32[1,64,64]{2,1,0:T(8,128)S(1)} %fusion.62), custom_call_target="InvertDiagBlocksLowerTriangular" | custom-call | tf_op jit(solution)/shard_map/jit(_cho_solve)/triangular_solve | solution.py:76
  (116 shorter events, 43.0 us)
Async XLA Ops:
  7.2 64.6 %all-gather.5.cloned.1.call-start = ((), (), s32[]{:S(2)}) async-start(), calls=%async_computation.4 | async-start | bytes 2359296 | tf_op jit(solution)/shard_map/all_gather | solution.py:61
  7.2 10.8 %collective-permute-start = (f32[64,1024]{1,0:T(8,128)}, f32[64,1024]{1,0:T(8,128)S(1)}, u32[]{:S(2)}, u32[]{:S(2)}) collective-permute-start(f32[64,1024]{1,0:T(8,128)} %param.9), channel_id=1, source_target_pairs={{0,1},{1,2},{2,3},{3,4},{4,5},{5,6},{6,7},{7,8},{8,9},{9,10},{10,1... | collective-permute-start | bytes 786440 | tf_op jit(solution)/shard_map/ppermute | solution.py:13
  14.1 12.0 %copy-start.8 = (f32[8,8]{1,0:T(8,128)}, f32[8,8]{1,0:T(8,128)S(1)}, u32[]{:S(2)}) copy-start(f32[8,8]{1,0:T(8,128)S(1)} %fusion.79) | copy-start | bytes 772
  19.3 2.2 copy-start
  28.7 11.6 %copy-start.10 = (s32[4,1,8]{2,1,0:T(1,128)S(1)}, s32[4,1,8]{2,1,0:T(1,128)}, u32[]{:S(2)}) copy-start(s32[4,1,8]{2,1,0:T(1,128)} %param.12) | copy-start | bytes 388
  29.0 10.0 %collective-permute-start.1 = (f32[64,1024]{1,0:T(8,128)S(1)}, f32[64,1024]{1,0:T(8,128)S(1)}, u32[]{:S(2)}, u32[]{:S(2)}) collective-permute-start(f32[64,1024]{1,0:T(8,128)S(1)} %bitcast.322), channel_id=1, source_target_pairs={{1,0},{2,1},{3,2},{4,3},{5,4},{6,5},{7,6},{8,7},{9,8},{10,9},{11,1... | collective-permute-start | bytes 786440 | tf_op jit(solution)/shard_map/ppermute | solution.py:13
  39.8 66.0 %reduce-scatter.3.cloned.1.call-start = ((), (), s32[]{:S(2)}) async-start(), calls=%async_computation.2 | async-start | bytes 1310720 | tf_op jit(solution)/shard_map/reduce_scatter | solution.py:70
  77.2 1.2 copy-start.2
  78.3 147.7 %all-gather.7.cloned.1.call-start = ((), (), s32[]{:S(2)}) async-start(), calls=%async_computation.5 | async-start | bytes 2359296 | tf_op jit(solution)/shard_map/all_gather | solution.py:61
  110.6 0.7 copy-start.4
  166.6 8.6 %copy-start.6 = (f32[64,1024]{1,0:T(8,128)}, f32[64,1024]{1,0:T(8,128)S(1)}, u32[]{:S(2)}) copy-start(f32[64,1024]{1,0:T(8,128)S(1)} %convolution_subtract_fusion.1) | copy-start | bytes 786436
  166.6 8.5 %collective-permute-start.2 = (f32[64,1024]{1,0:T(8,128)S(1)}, f32[64,1024]{1,0:T(8,128)S(1)}, u32[]{:S(2)}, u32[]{:S(2)}) collective-permute-start(f32[64,1024]{1,0:T(8,128)S(1)} %convolution_subtract_fusion.1), channel_id=1, source_target_pairs={{0,1},{1,2},{2,3},{3,4},{4,5},{5,6},{6,7},{7,8},{8,9},{9,10},{10,1... | collective-permute-start | bytes 786440 | tf_op jit(solution)/shard_map/ppermute | solution.py:13
  175.4 2.2 copy-start.1
  175.5 2.2 copy-start.9
  185.2 10.4 %collective-permute-start.3 = (f32[64,1024]{1,0:T(8,128)S(1)}, f32[64,1024]{1,0:T(8,128)S(1)}, u32[]{:S(2)}, u32[]{:S(2)}) collective-permute-start(f32[64,1024]{1,0:T(8,128)S(1)} %bitcast.323), channel_id=1, source_target_pairs={{1,0},{2,1},{3,2},{4,3},{5,4},{6,5},{7,6},{8,7},{9,8},{10,9},{11,1... | collective-permute-start | bytes 786440 | tf_op jit(solution)/shard_map/ppermute | solution.py:13
  196.3 63.8 %reduce-scatter.5.cloned.1.call-start = ((), (), s32[]{:S(2)}) async-start(), calls=%async_computation.3 | async-start | bytes 1310720 | tf_op jit(solution)/shard_map/reduce_scatter | solution.py:70
  231.5 13.3 %copy-start.3 = (f32[64,1024]{1,0:T(8,128)S(1)}, f32[64,1024]{1,0:T(8,128)}, u32[]{:S(2)}) copy-start(f32[64,1024]{1,0:T(8,128)} %bitcast_add_fusion) | copy-start | bytes 786436
  231.5 13.3 %copy-start.7 = (f32[64,1024]{1,0:T(8,128)S(1)}, f32[64,1024]{1,0:T(8,128)}, u32[]{:S(2)}) copy-start(f32[64,1024]{1,0:T(8,128)} %copy-done.6) | copy-start | bytes 786436
  245.2 61.0 %copy-start.5 = (f32[64,1024]{1,0:T(8,128)S(1)}, f32[64,1024]{1,0:T(8,128)}, u32[]{:S(2)}) copy-start(f32[64,1024]{1,0:T(8,128)} %copy-done.4) | copy-start | bytes 786436
Sparse Core Ops, SparseCore 0:
  39.9 31.7 all-gather.4
  78.4 27.2 reduce-scatter.2
  196.4 29.5 all-gather.6
  232.7 27.3 reduce-scatter.4
